TPU v7x, 32 devices: a whole 2x2x4 slice. The times are simulated.
32 devices in a mesh: section: 4 (over z), tensor: 8 (over y, x, core).
Axes of the slice: x: 2, y: 2, z: 4, core: 2. Of those that a mesh axis runs over, the one named last changes fastest.
Arguments:
- resid: bfloat16 [32, 3584], P('tensor'), may hold values from -6 to 6
- w_enc: bfloat16 [7168, 3584], P(('section', 'tensor')), may hold values from -0.09375 to 0.09375
- b_enc: float32 [7168], P(('section', 'tensor')), may hold values from -1 to 0.5
- w_dec: bfloat16 [7168, 3584], P(('section', 'tensor')), may hold values from -0.0625 to 0.0625
- b_dec: float32 [3584], replicated, may hold values from -3 to 3
Outputs:
- recon: float32 [32, 3584], P('tensor')
- grad_w_dec: bfloat16 [7168, 3584], P(('section', 'tensor'))
- code_grad: float32 [32, 7168], P(None, ('section', 'tensor'))
- grad_b_dec: float32 [3584], replicated
- loss_value: float32 [], replicated
All inputs are finite; a program needn't handle non-finite values.
Results may differ from a plain program's by a relative error of at most 0.0032.
The roundings to bfloat16 on the way count: a program that leaves them out, or rounds other values in their place, can miss the bound.
Values may be sent and summed in bfloat16 or wider, within the bound.
No kernel may reach another device: no remote copies, remote signals or barrier semaphores. Data moves between devices by JAX's collectives and lax.ppermute only.
A program may use at most 64 MiB of HBM per device.

v0:
```python
import jax
import jax.numpy as jnp
from jax import lax
from jax.sharding import PartitionSpec as P

epsilon = 1e-06


def per_device(resid, w_enc, b_enc, w_dec, b_dec):
    stream = lax.all_gather(resid, "tensor", axis=0, tiled=True)
    preact = (
        lax.dot_general(stream, w_enc, (((1,), (1,)), ((), ())), preferred_element_type=jnp.float32)
        + b_enc
    )
    codes = jnp.maximum(preact, 0.0).astype(jnp.bfloat16)
    codes_f32 = codes.astype(jnp.float32)
    dec_f32 = w_dec.astype(jnp.float32)
    dec_norm = jnp.sqrt(jnp.sum(dec_f32 * dec_f32, axis=1) + epsilon)
    penalty = lax.psum(jnp.sum(codes_f32 * dec_norm), ("section", "tensor"))
    total_rows = stream.shape[0]
    model_width = stream.shape[1]
    shares = lax.psum_scatter(
        jnp.dot(codes, w_dec, preferred_element_type=jnp.float32),
        "tensor",
        scatter_dimension=0,
        tiled=True,
    )
    shares = lax.psum(shares, "section")
    recon = shares + b_dec
    errors = recon - resid.astype(jnp.float32)
    squares, grad_b_dec = lax.psum((jnp.sum(errors * errors), jnp.sum(errors, axis=0)), "tensor")
    err_half = lax.all_gather(errors.astype(jnp.bfloat16), "tensor", axis=0, tiled=True)
    loss_value = (0.5 * squares + penalty) / (total_rows * model_width)
    code_sums = jnp.sum(codes_f32, axis=0)
    grad_w_dec = lax.dot_general(
        codes, err_half, (((0,), (0,)), ((), ())), preferred_element_type=jnp.float32
    )
    grad_w_dec = grad_w_dec + code_sums[:, None] * dec_f32 / dec_norm[:, None]
    code_grad = (
        lax.dot_general(
            err_half, w_dec, (((1,), (1,)), ((), ())), preferred_element_type=jnp.float32
        )
        + dec_norm
    )
    return (recon, grad_w_dec.astype(jnp.bfloat16), code_grad, grad_b_dec, loss_value)


def solution(mesh):
    in_specs = (
        P("tensor", None),
        P(("section", "tensor"), None),
        P(("section", "tensor")),
        P(("section", "tensor"), None),
        P(),
    )
    out_specs = (
        P("tensor", None),
        P(("section", "tensor"), None),
        P(None, ("section", "tensor")),
        P(),
        P(),
    )
    return jax.shard_map(
        per_device, mesh=mesh, in_specs=in_specs, out_specs=out_specs, check_vma=False
    )
```

profile of v0, /device:TPU:0, one launch (start us, length us, event | category | flops | bytes accessed | tf_op | source)
XLA Modules:
  0.0 148.7 jit_solution(17115211651597049739)
XLA Ops:
  7.2 0.0 copy-start
  7.2 0.0 copy-start.2
  7.2 0.0 copy-start.6
  7.2 0.0 all-reduce.4.cloned.1.call-start
  7.2 1.9 %fusion.2 = f32[224]{0:T(256)S(1)} fusion(bf16[224,3584]{1,0:T(8,128)(2,1)} %param.8), kind=kLoop, calls=%fused_computation.5 | loop fusion | flops 2408224 | bytes 1606528 | tf_op jit(solution)/shard_map/reduce_sum | solution.py:18
  9.2 0.0 copy-start.1
  9.2 0.0 copy-done.2
  9.2 12.0 %all-gather = bf16[8,4,3584]{2,1,0:T(4,128)(2,1)} all-gather(bf16[1,4,3584]{2,1,0:T(4,128)(2,1)S(1)} %bitcast.12), channel_id=1, replica_groups=mesh['section'=4,'tensor'=8] {'tensor'}, dimensions={0}, use_global_device_ids=true | all-gather | bytes 258048 | tf_op jit(solution)/shard_map/all_gather | solution.py:10
  21.2 1.0 reshape.22
  22.2 0.0 copy-done
  22.2 0.0 copy-done.6
  22.2 1.2 fusion.5
  23.4 0.0 copy-start.7
  23.4 0.0 copy-start.5
  23.4 0.0 copy-done.1
  23.4 1.2 fusion.7
  24.5 0.0 all-reduce.4.cloned.1.call-update
  24.5 39.9 %psum.31 = f32[]{:T(128)} all-reduce(f32[]{:T(128)} %get-tuple-element.7), channel_id=1, replica_groups=mesh['section'=4,'tensor'=8] {'section','tensor'}, use_global_device_ids=true, to_apply=%region_9.0 | all-reduce | flops 1 | bytes 8 | tf_op jit(solution)/shard_map/psum | solution.py:19
  64.4 0.0 copy-done.7
  64.4 0.6 dynamic-slice
  65.7 14.0 %all-reduce.4.cloned.1.call-done = f32[32,3584]{1,0:T(8,128)} async-done(((f32[32,3584]{1,0:T(8,128)}), f32[32,3584]{1,0:T(8,128)}) %all-reduce.4.cloned.1.call-update) | async-done | bytes 458768
  79.7 0.9 constant_dynamic-slice_fusion
  80.6 19.6 %psum.28 = f32[4,3584]{1,0:T(4,128)S(1)} all-reduce(f32[4,3584]{1,0:T(4,128)S(1)} %constant_dynamic-slice_fusion), channel_id=1, replica_groups=mesh['section'=4,'tensor'=8] {'section'}, use_global_device_ids=true, to_apply=%region_1.0 | all-reduce | flops 14336 | bytes 114688 | tf_op jit(solution)/shard_map/psum | solution.py:28
  100.2 0.0 copy-done.5
  100.2 0.7 multiply_reduce_fusion
  101.0 9.6 %all-gather.1 = bf16[8,4,3584]{2,1,0:T(4,128)(2,1)} all-gather(bf16[1,4,3584]{2,1,0:T(4,128)(2,1)S(1)} %convert_bitcast_fusion), channel_id=1, replica_groups=mesh['section'=4,'tensor'=8] {'tensor'}, dimensions={0}, use_global_device_ids=true | all-gather | bytes 258048 | tf_op jit(solution)/shard_map/all_gather | solution.py:32
  110.6 1.0 reshape.24
  111.6 1.2 convolution_add_fusion.1
  112.8 1.8 %fusion = bf16[224,3584]{1,0:T(8,128)(2,1)} fusion(bf16[32,224]{1,0:T(8,128)(2,1)S(1)} %get-tuple-element.12, bf16[32,3584]{1,0:T(8,128)(2,1)S(1)} %reshape.24, bf16[224,3584]{1,0:T(8,128)(2,1)S(1)} %copy-done.1, f32[224]{0:T(256)S(1)} %add_sqrt_fusion, f32[224]{0:T(256)S(1)} %get-tuple-element.8), kind=kOutput, calls=%fused_computation.1 | convolution fusion | flops 55394304 | bytes 3456768 | tf_op jit(solution)/shard_map/dot_general | solution.py:35
  114.6 0.0 copy-done.3
  114.6 0.0 copy-done.4
  114.6 24.8 %all-reduce.1 = (f32[3584]{0:T(1024)}, f32[]{:T(128)}) all-reduce(f32[3584]{0:T(1024)S(1)} %copy-done.4, f32[]{:T(128)} %get-tuple-element.5), channel_id=1, replica_groups=mesh['section'=4,'tensor'=8] {'tensor'}, use_global_device_ids=true, to_apply=%region_5.0 | all-reduce | flops 3585 | bytes 28680 | tf_op jit(solution)/shard_map/psum | solution.py:31
  (4 shorter events, 0.0 us)
Async XLA Ops:
  7.2 15.0 %copy-start = (bf16[224,3584]{1,0:T(8,128)(2,1)S(1)}, bf16[224,3584]{1,0:T(8,128)(2,1)}, u32[]{:S(2)}) copy-start(bf16[224,3584]{1,0:T(8,128)(2,1)} %param.6) | copy-start | bytes 4816900
  7.2 2.0 %copy-start.2 = (bf16[4,3584]{1,0:T(4,128)(2,1)S(1)}, bf16[4,3584]{1,0:T(4,128)(2,1)}, u32[]{:S(2)}) copy-start(bf16[4,3584]{1,0:T(4,128)(2,1)} %param.5) | copy-start | bytes 86020
  7.2 15.0 %copy-start.6 = (f32[224]{0:T(256)S(1)}, f32[224]{0:T(256)}, u32[]{:S(2)}) copy-start(f32[224]{0:T(256)} %param.7) | copy-start | bytes 2692
  7.2 72.5 %all-reduce.4.cloned.1.call-start = ((), (), s32[]{:S(2)}) async-start(), calls=%async_computation | async-start | bytes 917504
  9.2 14.2 %copy-start.1 = (bf16[224,3584]{1,0:T(8,128)(2,1)S(1)}, bf16[224,3584]{1,0:T(8,128)(2,1)}, u32[]{:S(2)}) copy-start(bf16[224,3584]{1,0:T(8,128)(2,1)} %param.8) | copy-start | bytes 4816900
  23.4 41.1 %copy-start.7 = (u32[32]{0:T(128)S(1)}, u32[32]{0:T(128)}, u32[]{:S(2)}) copy-start(u32[32]{0:T(128)} %constant.13) | copy-start | bytes 388
  23.4 76.8 %copy-start.5 = (f32[3584]{0:T(1024)S(1)}, f32[3584]{0:T(1024)}, u32[]{:S(2)}) copy-start(f32[3584]{0:T(1024)} %param.9) | copy-start | bytes 43012
  100.9 13.6 %copy-start.3 = (f32[4,3584]{1,0:T(4,128)}, f32[4,3584]{1,0:T(4,128)S(1)}, u32[]{:S(2)}) copy-start(f32[4,3584]{1,0:T(4,128)S(1)} %get-tuple-element.11) | copy-start | bytes 172036
  112.8 1.8 %copy-start.4 = (f32[3584]{0:T(1024)S(1)}, f32[3584]{0:T(1024)}, u32[]{:S(2)}) copy-start(f32[3584]{0:T(1024)} %get-tuple-element.6) | copy-start | bytes 43012
Sparse Core Ops, SparseCore 0:
  24.7 54.9 all-reduce.3
where the time goes:
time: 149 us
  blocking collectives  106 us (71%)
  between operations  17.2 us (12%)
  waiting for transfers between devices  14 us (9%)
  matrix products  5.33 us (4%)
  local copies, waits for them, and re-layouts  3.52 us (2%)
  other arithmetic  2.7 us (2%)
    psum x1, blocking collectives, per_device(): penalty = lax.psum(jnp.sum(codes_f32 * dec_norm), ('section', 'tensor'))  39.9 us
    psum x1, blocking collectives, per_device(): lax.psum((jnp.sum(errors * errors), jnp.sum(errors, axis=0)), 'tensor')  24.8 us
    psum x1, blocking collectives, per_device(): shares = lax.psum(shares, 'section')  19.6 us
    unnamed x2, waiting for transfers between devices  14 us
    all_gather x1, blocking collectives, per_device(): stream = lax.all_gather(resid, 'tensor', axis=0, tiled=True)  12 us
    all_gather x1, blocking collectives, per_device(): lax.all_gather(errors.astype(jnp.bfloat16), 'tensor', axis=0, tiled=True)  9.61 us
    unnamed x20, local copies, waits for them, and re-layouts  3.52 us
  transfers between devices with their start and end apart: 1, of which 1 were waited for; matrix products, arithmetic and copies ran while one was open for 0% of the time, Pallas kernels for 0%

commit v1 on v0

--- a/solution.py
+++ b/solution.py
@@ -25,7 +25,9 @@
         scatter_dimension=0,
         tiled=True,
     )
-    shares = lax.psum(shares, "section")
+    shares = shares
+    for hop in (1, 2):
+        shares = shares + lax.ppermute(shares, "section", [(dev, dev ^ hop) for dev in range(4)])
     recon = shares + b_dec
     errors = recon - resid.astype(jnp.float32)
     squares, grad_b_dec = lax.psum((jnp.sum(errors * errors), jnp.sum(errors, axis=0)), "tensor")

time: 149 us -> 178 us (1.19)
  waiting for transfers between devices: 14 us -> 56.6 us
  blocking collectives: 106 us -> 87.4 us
  starting transfers between devices: 0.04 us -> 3.92 us
    unnamed x2, waiting for transfers between devices: 14 us -> 53.8 us
    psum x1 -> x0, blocking collectives: 19.6 us -> none  [per_device(): shares = lax.psum(shares, 'section')]
    ppermute x0 -> x2, starting transfers between devices: none -> 3.88 us  [per_device(): lax.ppermute(shares, 'section', [(dev, dev ^ hop) for dev in range(4)])]
    ppermute x0 -> x2, waiting for transfers between devices: none -> 2.76 us  [per_device(): lax.ppermute(shares, 'section', [(dev, dev ^ hop) for dev in range(4)])]
  transfers between devices with their start and end apart: 1 -> 3, of which waited for: 1 -> 2; matrix products, arithmetic and copies ran while one was open for 0% -> 0% of each run, Pallas kernels for 0% -> 0%
where the time goes in v1:
time: 178 us
  blocking collectives  87.4 us (49%)
  waiting for transfers between devices  56.6 us (32%)
  between operations  17.1 us (10%)
  matrix products  5.34 us (3%)
  starting transfers between devices  3.92 us (2%)
  other arithmetic  3.63 us (2%)
  local copies, waits for them, and re-layouts  3.52 us (2%)
    unnamed x2, waiting for transfers between devices  53.8 us
    psum x1, blocking collectives, per_device(): penalty = lax.psum(jnp.sum(codes_f32 * dec_norm), ('section', 'tensor'))  39.4 us
    psum x1, blocking collectives, per_device(): lax.psum((jnp.sum(errors * errors), jnp.sum(errors, axis=0)), 'tensor')  24.8 us
    all_gather x1, blocking collectives, per_device(): stream = lax.all_gather(resid, 'tensor', axis=0, tiled=True)  12 us
    all_gather x1, blocking collectives, per_device(): lax.all_gather(errors.astype(jnp.bfloat16), 'tensor', axis=0, tiled=True)  11.2 us
    ppermute x2, starting transfers between devices, per_device(): lax.ppermute(shares, 'section', [(dev, dev ^ hop) for dev in range(4)])  3.88 us
  transfers between devices with their start and end apart: 3, of which 2 were waited for; matrix products, arithmetic and copies ran while one was open for 0% of the time, Pallas kernels for 0%

profile of v1, /device:TPU:0, one launch (start us, length us, event | category | flops | bytes accessed | tf_op | source)
XLA Modules:
  0.0 177.5 jit_solution(13409253331796959370)
XLA Ops:
  7.2 0.0 copy-start
  7.2 0.0 copy-start.2
  7.2 0.0 copy-start.6
  7.2 0.0 all-reduce.4.cloned.1.call-start
  7.2 1.9 %fusion.2 = f32[224]{0:T(256)S(1)} fusion(bf16[224,3584]{1,0:T(8,128)(2,1)} %param.8), kind=kLoop, calls=%fused_computation.5 | loop fusion | flops 2408224 | bytes 1606528 | tf_op jit(solution)/shard_map/reduce_sum | solution.py:18
  9.2 0.0 copy-done.2
  9.2 12.0 %all-gather = bf16[8,4,3584]{2,1,0:T(4,128)(2,1)} all-gather(bf16[1,4,3584]{2,1,0:T(4,128)(2,1)S(1)} %bitcast.12), channel_id=1, replica_groups=mesh['section'=4,'tensor'=8] {'tensor'}, dimensions={0}, use_global_device_ids=true | all-gather | bytes 258048 | tf_op jit(solution)/shard_map/all_gather | solution.py:10
  21.2 1.0 reshape.22
  22.2 0.0 copy-done
  22.2 0.0 copy-done.6
  22.2 1.2 fusion.5
  23.4 0.0 copy-done.1
  23.4 1.2 fusion.7
  24.5 0.0 all-reduce.4.cloned.1.call-update
  24.6 0.0 copy-done.7
  24.6 0.6 dynamic-slice
  25.8 53.8 %all-reduce.4.cloned.1.call-done = f32[32,3584]{1,0:T(8,128)} async-done(((f32[32,3584]{1,0:T(8,128)}), f32[32,3584]{1,0:T(8,128)}) %all-reduce.4.cloned.1.call-update) | async-done | bytes 458768
  79.6 0.9 constant_dynamic-slice_fusion
  80.5 1.5 collective-permute-start
  82.0 2.8 %collective-permute-done = f32[4,3584]{1,0:T(4,128)S(1)} collective-permute-done((f32[4,3584]{1,0:T(4,128)S(1)}, f32[4,3584]{1,0:T(4,128)S(1)}, u32[]{:S(2)}, u32[]{:S(2)}) %collective-permute-start) | collective-permute-done | bytes 57376 | tf_op jit(solution)/shard_map/ppermute | solution.py:30
  84.8 0.9 fusion.16
  85.7 2.4 %collective-permute-start.1 = (f32[4,3584]{1,0:T(4,128)S(1)}, f32[4,3584]{1,0:T(4,128)S(1)}, u32[]{:S(2)}, u32[]{:S(2)}) collective-permute-start(f32[4,3584]{1,0:T(4,128)S(1)} %fusion.16), channel_id=1, source_target_pairs={{0,16},{8,24},{16,0},{24,8},{1,17},{9,25},{17,1},{25,9},{2,18},{10... | collective-permute-start | bytes 172040 | tf_op jit(solution)/shard_map/ppermute | solution.py:30
  88.1 39.4 %psum.23 = f32[]{:T(128)} all-reduce(f32[]{:T(128)} %get-tuple-element.7), channel_id=1, replica_groups=mesh['section'=4,'tensor'=8] {'section','tensor'}, use_global_device_ids=true, to_apply=%region_8.0 | all-reduce | flops 1 | bytes 8 | tf_op jit(solution)/shard_map/psum | solution.py:19
  127.5 0.0 collective-permute-done.1
  127.5 0.0 copy-done.5
  127.5 0.8 multiply_reduce_fusion
  128.3 11.2 %all-gather.1 = bf16[8,4,3584]{2,1,0:T(4,128)(2,1)} all-gather(bf16[1,4,3584]{2,1,0:T(4,128)(2,1)S(1)} %convert_bitcast_fusion), channel_id=1, replica_groups=mesh['section'=4,'tensor'=8] {'tensor'}, dimensions={0}, use_global_device_ids=true | all-gather | bytes 258048 | tf_op jit(solution)/shard_map/all_gather | solution.py:34
  139.5 1.0 reshape.24
  140.5 1.2 convolution_add_fusion.1
  141.7 1.8 %fusion = bf16[224,3584]{1,0:T(8,128)(2,1)} fusion(bf16[32,224]{1,0:T(8,128)(2,1)S(1)} %get-tuple-element.12, bf16[32,3584]{1,0:T(8,128)(2,1)S(1)} %reshape.24, bf16[224,3584]{1,0:T(8,128)(2,1)S(1)} %copy-done.1, f32[224]{0:T(256)S(1)} %add_sqrt_fusion, f32[224]{0:T(256)S(1)} %get-tuple-element.8), kind=kOutput, calls=%fused_computation.1 | convolution fusion | flops 55394304 | bytes 3456768 | tf_op jit(solution)/shard_map/dot_general | solution.py:37
  143.5 0.0 copy-done.3
  143.5 24.8 %all-reduce.1 = (f32[3584]{0:T(1024)}, f32[]{:T(128)}) all-reduce(f32[3584]{0:T(1024)S(1)} %copy-done.4, f32[]{:T(128)} %get-tuple-element.5), channel_id=1, replica_groups=mesh['section'=4,'tensor'=8] {'tensor'}, use_global_device_ids=true, to_apply=%region_4.0 | all-reduce | flops 3585 | bytes 28680 | tf_op jit(solution)/shard_map/psum | solution.py:33
  (8 shorter events, 0.0 us)
Async XLA Ops:
  7.2 15.0 %copy-start = (bf16[224,3584]{1,0:T(8,128)(2,1)S(1)}, bf16[224,3584]{1,0:T(8,128)(2,1)}, u32[]{:S(2)}) copy-start(bf16[224,3584]{1,0:T(8,128)(2,1)} %param.6) | copy-start | bytes 4816900
  7.2 2.0 %copy-start.2 = (bf16[4,3584]{1,0:T(4,128)(2,1)S(1)}, bf16[4,3584]{1,0:T(4,128)(2,1)}, u32[]{:S(2)}) copy-start(bf16[4,3584]{1,0:T(4,128)(2,1)} %param.5) | copy-start | bytes 86020
  7.2 15.0 %copy-start.6 = (f32[224]{0:T(256)S(1)}, f32[224]{0:T(256)}, u32[]{:S(2)}) copy-start(f32[224]{0:T(256)} %param.7) | copy-start | bytes 2692
  7.2 72.4 %all-reduce.4.cloned.1.call-start = ((), (), s32[]{:S(2)}) async-start(), calls=%async_computation | async-start | bytes 917504
  9.2 14.2 %copy-start.1 = (bf16[224,3584]{1,0:T(8,128)(2,1)S(1)}, bf16[224,3584]{1,0:T(8,128)(2,1)}, u32[]{:S(2)}) copy-start(bf16[224,3584]{1,0:T(8,128)(2,1)} %param.8) | copy-start | bytes 4816900
  23.4 1.2 copy-start.7
  23.4 104.1 %copy-start.5 = (f32[3584]{0:T(1024)S(1)}, f32[3584]{0:T(1024)}, u32[]{:S(2)}) copy-start(f32[3584]{0:T(1024)} %param.9) | copy-start | bytes 43012
  80.5 4.2 %collective-permute-start = (f32[4,3584]{1,0:T(4,128)S(1)}, f32[4,3584]{1,0:T(4,128)S(1)}, u32[]{:S(2)}, u32[]{:S(2)}) collective-permute-start(f32[4,3584]{1,0:T(4,128)S(1)} %constant_dynamic-slice_fusion), channel_id=1, source_target_pairs={{0,8},{8,0},{16,24},{24,16},{1,9},{9,1},{17,25},{25,17},{2,10},{10... | collective-permute-start | bytes 172040 | tf_op jit(solution)/shard_map/ppermute | solution.py:30
  85.7 41.8 %collective-permute-start.1 = (f32[4,3584]{1,0:T(4,128)S(1)}, f32[4,3584]{1,0:T(4,128)S(1)}, u32[]{:S(2)}, u32[]{:S(2)}) collective-permute-start(f32[4,3584]{1,0:T(4,128)S(1)} %fusion.16), channel_id=1, source_target_pairs={{0,16},{8,24},{16,0},{24,8},{1,17},{9,25},{17,1},{25,9},{2,18},{10... | collective-permute-start | bytes 172040 | tf_op jit(solution)/shard_map/ppermute | solution.py:30
  128.3 15.3 %copy-start.3 = (f32[4,3584]{1,0:T(4,128)}, f32[4,3584]{1,0:T(4,128)S(1)}, u32[]{:S(2)}) copy-start(f32[4,3584]{1,0:T(4,128)S(1)} %get-tuple-element.11) | copy-start | bytes 172036
  141.7 1.8 %copy-start.4 = (f32[3584]{0:T(1024)S(1)}, f32[3584]{0:T(1024)}, u32[]{:S(2)}) copy-start(f32[3584]{0:T(1024)} %get-tuple-element.6) | copy-start | bytes 43012
Sparse Core Ops, SparseCore 0:
  24.7 54.9 all-reduce.3
